TPU v7x, 256 devices: a whole 4x4x8 slice. The times are simulated.
256 devices in a mesh: expert: 8 (over x, core), latent: 32 (over y, z).
Axes of the slice: x: 4, y: 4, z: 8, core: 2. Of those that a mesh axis runs over, the one named last changes fastest.
Arguments:
- tokens: bfloat16 [2048, 2560], P(('expert', 'latent')), may hold values from -6 to 6
- route: int32 [2048, 1], P(('expert', 'latent')), may hold values from 0 to 7; in each aligned block of 8 rows (0 to 7, 8 to 15, ...) at most 2 rows name the same one
- blocks: int32 [2048, 64], P(('expert', 'latent')), may hold values from 0 to 255, all different within a row
- weight: bfloat16 [8, 2560, 32768], P('expert', None, 'latent'), may hold values from -0.125 to 0.125
- enc_bias: float32 [8, 32768], P('expert', 'latent'), may hold values from -3 to 3
- dec_bias: float32 [2560], replicated, may hold values from -3 to 3
Outputs:
- grad_weight: bfloat16 [8, 2560, 32768], P('expert', None, 'latent')
- grad_enc: float32 [8, 32768], P('expert', 'latent')
- grad_dec: float32 [2560], replicated
- loss: float32 [], replicated
Inputs may be any that keep to these rules, and one draw needn't show every extreme that they name: `route`: within the rows of one device (aligned blocks of 8 rows) no expert is named by more than 2 rows. Each row lists 64 different blocks.
All inputs are finite; a program needn't handle non-finite values.
Results may differ from a plain program's by a relative error of at most 0.012.
The roundings to bfloat16 on the way count: a program that leaves them out, or rounds other values in their place, can miss the bound.
Values may be sent and summed in bfloat16 or wider, within the bound.
No kernel may reach another device: no remote copies, remote signals or barrier semaphores. Data moves between devices by JAX's collectives and lax.ppermute only.
A program may use at most 128 MiB of HBM per device.

v0:
```python
import jax
import jax.numpy as jnp
from jax import lax
from jax.sharding import PartitionSpec as P

BLK = 128
CAP = 2


def shards(tokens, route, blocks, weight, enc_bias, dec_bias):
    n_expert = lax.axis_size("expert")
    n_latent = lax.axis_size("latent")
    width = tokens.shape[1]
    list_len = blocks.shape[1]
    expert_of = route[:, 0]
    one_hot = (expert_of[:, None] == jnp.arange(n_expert, dtype=jnp.int32)[None, :]).astype(
        jnp.int32
    )
    earlier = jnp.sum((jnp.cumsum(one_hot, axis=0) - one_hot) * one_hot, axis=1)
    target = expert_of * CAP + earlier
    send_rows = jnp.zeros((n_expert * CAP, width), jnp.bfloat16).at[target].set(tokens)
    send_rows = send_rows.reshape(n_expert, CAP, width)
    send_lists = jnp.full((n_expert * CAP, list_len), -1, jnp.int32).at[target].set(blocks)
    send_lists = send_lists.reshape(n_expert, CAP, list_len)
    got_rows, got_lists = (
        lax.all_to_all(send_rows, "expert", split_axis=0, concat_axis=0, tiled=True),
        lax.all_to_all(send_lists, "expert", split_axis=0, concat_axis=0, tiled=True),
    )
    all_rows, all_lists = (
        lax.all_gather(got_rows[None], "latent", axis=0, tiled=True),
        lax.all_gather(got_lists[None], "latent", axis=0, tiled=True),
    )
    token_rows = all_rows.reshape(-1, width)
    listed = all_lists.reshape(-1, list_len)
    row_count = token_rows.shape[0]
    valid = (listed[:, 0] >= 0).astype(jnp.float32)
    slice_index = lax.axis_index("latent")
    weights_here = weight[0]
    per_slice = weights_here.shape[1] // BLK
    own_blocks = slice_index * per_slice + jnp.arange(per_slice, dtype=jnp.int32)
    chosen = jnp.any(listed[:, :, None] == own_blocks[None, None, :], axis=1).astype(jnp.float32)
    mask = jnp.repeat(chosen, BLK, axis=1)
    rows_f32 = token_rows.astype(jnp.float32)
    shifted = (rows_f32 - dec_bias).astype(jnp.bfloat16)
    pre_act = jnp.dot(shifted, weights_here, preferred_element_type=jnp.float32) + enc_bias[0]
    active = jnp.maximum(pre_act, 0.0) * mask
    active_bf = active.astype(jnp.bfloat16)
    share = row_count // n_latent
    first_row = slice_index * share
    along_width = (((1,), (1,)), ((), ()))
    partial_sum = lax.dot_general(
        active_bf, weights_here, along_width, preferred_element_type=jnp.float32
    )
    summed = lax.psum(partial_sum, "latent")
    error_all = (summed + dec_bias - rows_f32) * valid[:, None]
    error_bf = error_all.astype(jnp.bfloat16)
    error_share = lax.dynamic_slice_in_dim(error_all, first_row, share, 0)
    grad_act = jnp.dot(error_bf, weights_here, preferred_element_type=jnp.float32)
    grad_pre = grad_act * (pre_act > 0.0).astype(jnp.float32) * mask
    grad_pre_bf = grad_pre.astype(jnp.bfloat16)
    along_rows = (((0,), (0,)), ((), ()))
    grad_here = lax.dot_general(
        shifted, grad_pre_bf, along_rows, preferred_element_type=jnp.float32
    )
    grad_here = grad_here + lax.dot_general(
        error_bf, active_bf, along_rows, preferred_element_type=jnp.float32
    )
    grad_bias = jnp.sum(grad_pre, axis=0)
    pulled = jnp.dot(
        weights_here, grad_bias.astype(jnp.bfloat16), preferred_element_type=jnp.float32
    )
    bias_term = jnp.sum(error_share, axis=0) - pulled
    loss_term = 0.5 * jnp.sum(error_share * error_share)
    grad_dec, loss_sum = lax.psum((bias_term, loss_term), ("expert", "latent"))
    loss = loss_sum / (tokens.shape[0] * n_expert * n_latent)
    return (grad_here.astype(jnp.bfloat16)[None], grad_bias[None], grad_dec, loss)


def solution(mesh):
    return jax.shard_map(
        shards,
        mesh=mesh,
        in_specs=(
            P(("expert", "latent"), None),
            P(("expert", "latent"), None),
            P(("expert", "latent"), None),
            P("expert", None, "latent"),
            P("expert", "latent"),
            P(),
        ),
        out_specs=(P("expert", None, "latent"), P("expert", "latent"), P(), P()),
        check_vma=False,
    )
```

profile of v0, /device:TPU:1, one launch (start us, length us, event | category | flops | bytes accessed | tf_op | source)
XLA Modules:
  0.0 402.3 jit_solution(3232776257881222928)
XLA Ops:
  7.2 0.7 fusion.24
  8.0 0.8 select_reduce_fusion
  8.8 0.7 fusion.25
  9.5 0.9 scatter_custom_fusion
  10.4 11.2 %all_to_all.10 = bf16[8,2,2560]{2,1,0:T(2,128)(2,1)} all-to-all(bf16[8,2,2560]{2,1,0:T(2,128)(2,1)S(1)} %reshape.33), channel_id=1, replica_groups=mesh['expert'=8,'latent'=32] {'expert'}, dimensions={0} | all-to-all | bytes 163840 | tf_op jit(solution)/shard_map/all_to_all | solution.py:26
  21.7 0.8 scatter_custom_fusion.1
  22.4 0.7 reshape.68
  23.1 4.0 all-to-all-start.1
  27.1 4.5 %all-to-all-done.1 = s32[8,1,128]{2,1,0:T(1,128)S(1)} async-done(((s32[8,1,128]{2,1,0:T(1,128)}), s32[8,1,128]{2,1,0:T(1,128)S(1)}, u32[]{:S(2)}, u32[]{:S(2)}) %all-to-all-start.1) | async-done | bytes 4128 | tf_op jit(solution)/shard_map/all_to_all | solution.py:27
  31.6 0.5 broadcast.43
  32.2 0.7 reduce.4
  32.9 40.8 %all-gather.1 = s32[256,2,64]{2,1,0:T(2,128)S(1)} all-gather(s32[8,2,64]{2,1,0:T(2,128)S(1)} %reshape.69), channel_id=3, replica_groups=mesh['expert'=8,'latent'=32] {'latent'}, dimensions={0}, use_global_device_ids=true | all-gather | bytes 135168 | tf_op jit(solution)/shard_map/all_gather | solution.py:31
  73.8 0.2 compare_reduce_fusion
  74.1 0.1 copy.13
  74.2 24.0 %all-gather.4.cloned.1.call-done = bf16[256,2,2560]{2,1,0:T(2,128)(2,1)} async-done(((bf16[8,2,2560]{2,1,0:T(2,128)(2,1)}), bf16[256,2,2560]{2,1,0:T(2,128)(2,1)}) %all-gather.4.cloned.1.call-update) | async-done | bytes 2621456 | tf_op jit(solution)/shard_map/all_gather | solution.py:30
  98.1 3.5 convert_element_type.56
  101.7 2.3 subtract_convert_fusion
  104.0 2.6 convert_element_type.47
  106.6 0.6 broadcast_in_dim.32
  107.3 8.7 %fusion.11 = (bf16[512,1024]{1,0:T(8,128)(2,1)S(1)}, f32[512,1024]{1,0:T(8,128)}) fusion(f32[64,8,8,128]{3,2,1,0:T(8,128)S(1)} %bitcast.51, f32[1024]{0:T(1024)S(1)} %bitcast.57, bf16[512,2560]{1,0:T(8,128)(2,1)} %convert_element_type.47, bf16[1,2560,1024]{2,1,0:T(8,128)(2,1)} %param.9), kind=kOutput, calls=%fused_computation.19 | convolution fusion | flops 2686451712 | bytes 13111296 | tf_op jit(solution)/shard_map/dot_general | solution.py:45
  116.0 1.0 copy-done.3
  117.0 4.7 %fusion.4 = f32[512,2560]{1,0:T(8,128)} fusion(bf16[512,1024]{1,0:T(8,128)(2,1)S(1)} %get-tuple-element.8, bf16[1,2560,1024]{2,1,0:T(8,128)(2,1)S(1)} %bitcast.46), kind=kOutput, calls=%fused_computation.7 | convolution fusion | flops 2684354560 | bytes 11534336 | tf_op jit(solution)/shard_map/dot_general | solution.py:51
  121.8 1.6 copy-done
  123.4 2.9 reshape.36
  126.4 168.2 %all-reduce.3.cloned.1.call-done = f32[512,2560]{1,0:T(8,128)} async-done(((f32[512,2560]{1,0:T(8,128)}), f32[512,2560]{1,0:T(8,128)}) %all-reduce.3.cloned.1.call-update) | async-done | bytes 5242896 | tf_op jit(solution)/shard_map/psum | solution.py:54
  294.5 4.9 %subtract_multiply_fusion = f32[512,2560]{1,0:T(8,128)S(1)} fusion(f32[512,2560]{1,0:T(8,128)} %reshape.36, f32[512,2560]{1,0:T(8,128)} %all-reduce.3.cloned.1.call-done, f32[512]{0:T(512)S(1)} %convert_reduce_fusion, f32[2560]{0:T(1024)S(1)} %copy-done.4), kind=kLoop, calls=%fused_computation.11 | loop fusion | flops 3932160 | bytes 15740928 | tf_op jit(solution)/shard_map/mul | solution.py:55
  299.5 5.9 %fusion.26 = (f32[1024]{0:T(1024)S(1)}, bf16[512,1024]{1,0:T(8,128)(2,1)S(1)}) fusion(f32[64,8,8,128]{3,2,1,0:T(8,128)S(1)} %bitcast.52, bf16[1,2560,1024]{2,1,0:T(8,128)(2,1)} %param.9, f32[512,2560]{1,0:T(8,128)S(1)} %subtract_multiply_fusion, f32[512,1024]{1,0:T(8,128)S(1)} %copy-done.7, f32[1024]{0:T(1024)S(1)} %bitcast.58), kind=kOutput, calls=%fused_computation.40 | convolution fusion | flops 2688809984 | bytes 15736832 | tf_op jit(solution)/shard_map/dot_general | solution.py:58
  305.5 3.0 fusion.9
  308.5 6.5 %fusion.8 = bf16[1,2560,1024]{2,1,0:T(8,128)(2,1)} fusion(f32[2560,1024]{1,0:T(8,128)S(1)} %fusion.9, bf16[512,1024]{1,0:T(8,128)(2,1)} %copy-done.3, f32[512,2560]{1,0:T(8,128)S(1)} %subtract_multiply_fusion), kind=kOutput, calls=%fused_computation.14 | convolution fusion | flops 2690908160 | bytes 22020096 | tf_op jit(solution)/shard_map/dot_general | solution.py:65
  315.0 0.6 multiply_reduce_fusion
  315.6 1.5 fusion.16
  317.8 75.9 %all-reduce = (f32[2560]{0:T(1024)}, f32[]{:T(128)}) all-reduce(f32[2560]{0:T(1024)S(1)} %sub.28, f32[]{:T(128)S(6)} %mul_shard_map.3), channel_id=1, replica_groups=mesh['expert'=8,'latent'=32] {'expert','latent'}, use_global_device_ids=true, to_apply=%region_8.9 | all-reduce | flops 2561 | bytes 20488 | tf_op jit(solution)/shard_map/psum | solution.py:74
  (43 shorter events, 0.5 us)
Async XLA Ops:
  7.2 94.5 %copy-start.4 = (f32[2560]{0:T(1024)S(1)}, f32[2560]{0:T(1024)}, u32[]{:S(2)}) copy-start(f32[2560]{0:T(1024)} %param.11) | copy-start | bytes 30724
  7.2 91.0 %all-gather.4.cloned.1.call-start = ((), (), s32[]{:S(2)}) async-start(), calls=%async_computation.3 | async-start | bytes 2703360 | tf_op jit(solution)/shard_map/all_gather | solution.py:30
  23.1 8.5 %all-to-all-start.1 = ((s32[8,1,128]{2,1,0:T(1,128)}), s32[8,1,128]{2,1,0:T(1,128)S(1)}, u32[]{:S(2)}, u32[]{:S(2)}) async-start(s32[8,1,128]{2,1,0:T(1,128)} %reshape.68), calls=%async_computation.1 | async-start | bytes 8192 | tf_op jit(solution)/shard_map/all_to_all | solution.py:27
  27.1 267.4 %all-reduce.3.cloned.1.call-start = ((), (), s32[]{:S(2)}) async-start(), calls=%async_computation.2 | async-start | bytes 10485760 | tf_op jit(solution)/shard_map/psum | solution.py:54
  104.0 3.2 copy-start.6
  106.6 10.4 %slice-start.2 = ((s8[5242880]{0:T(1024)(128)(4,1)}), s8[4194304]{0:T(1024)(128)(4,1)S(1)}, s32[]{:S(2)}) async-start(s8[5242880]{0:T(1024)(128)(4,1)} %bitcast.45), calls=%async_computation.6 | async-start | bytes 8388608
  107.2 8.8 %copy-start.1 = (f32[512,8,128]{2,1,0:T(8,128)}, f32[512,8,128]{2,1,0:T(8,128)S(1)}, u32[]{:S(2)}) copy-start(f32[512,8,128]{2,1,0:T(8,128)S(1)} %broadcast_in_dim.32) | copy-start | bytes 6291460
  107.2 9.7 %slice-start.3 = ((s8[5242880]{0:T(1024)(128)(4,1)}), s8[1048576]{0:T(1024)(128)(4,1)S(1)}, s32[]{:S(2)}) async-start(s8[5242880]{0:T(1024)(128)(4,1)} %bitcast.45), calls=%async_computation.7 | async-start | bytes 2097152
  116.0 1.0 copy-start.3
  121.7 1.7 copy-start
  126.3 173.1 %copy-start.2 = (f32[512,8,128]{2,1,0:T(8,128)S(1)}, f32[512,8,128]{2,1,0:T(8,128)}, u32[]{:S(2)}) copy-start(f32[512,8,128]{2,1,0:T(8,128)} %copy-done.1) | copy-start | bytes 6291460
  294.5 4.9 %copy-start.7 = (f32[512,1024]{1,0:T(8,128)S(1)}, f32[512,1024]{1,0:T(8,128)}, u32[]{:S(2)}) copy-start(f32[512,1024]{1,0:T(8,128)} %get-tuple-element.9) | copy-start | bytes 6291460
  294.5 10.9 %slice-start = ((s8[5242880]{0:T(1024)(128)(4,1)}), s8[1048576]{0:T(1024)(128)(4,1)S(1)}, s32[]{:S(2)}) async-start(s8[5242880]{0:T(1024)(128)(4,1)} %bitcast.42), calls=%async_computation.4 | async-start | bytes 2097152
  299.5 6.0 %slice-start.1 = ((s8[5242880]{0:T(1024)(128)(4,1)}), s8[4194304]{0:T(1024)(128)(4,1)S(1)}, s32[]{:S(2)}) async-start(s8[5242880]{0:T(1024)(128)(4,1)} %bitcast.42), calls=%async_computation.5 | async-start | bytes 8388608
  305.4 10.2 %copy-start.5 = (f32[1024]{0:T(1024)}, f32[1024]{0:T(1024)S(1)}, u32[]{:S(2)}) copy-start(f32[1024]{0:T(1024)S(1)} %get-tuple-element.10) | copy-start | bytes 12292
  305.4 10.2 %slice-start.4 = ((s8[5242880]{0:T(1024)(128)(4,1)}), s8[4194304]{0:T(1024)(128)(4,1)S(1)}, s32[]{:S(2)}) async-start(s8[5242880]{0:T(1024)(128)(4,1)} %bitcast.47), calls=%async_computation.8 | async-start | bytes 8388608
  308.5 7.2 %slice-start.5 = ((s8[5242880]{0:T(1024)(128)(4,1)}), s8[1048576]{0:T(1024)(128)(4,1)S(1)}, s32[]{:S(2)}) async-start(s8[5242880]{0:T(1024)(128)(4,1)} %bitcast.47), calls=%async_computation.9 | async-start | bytes 2097152
Sparse Core Ops, SparseCore 0:
  21.8 76.3 all-gather.3
  121.8 172.6 all-reduce.2
where the time goes:
time: 403 us; the launch traced here: 402 us
  waiting for transfers between devices  197 us (49%)
  blocking collectives  128 us (32%)
  matrix products  30.3 us (8%)
  between operations  16.7 us (4%)
  other arithmetic  14.6 us (4%)
  local copies, waits for them, and re-layouts  12 us (3%)
  starting transfers between devices  4.05 us (1%)
    psum x1, waiting for transfers between devices, shards(): summed = lax.psum(partial_sum, 'latent')  168 us
    psum x1, blocking collectives, shards(): grad_dec, loss_sum = lax.psum((bias_term, loss_term), ('expert', 'latent'))  75.9 us
    all_gather x1, blocking collectives, shards(): lax.all_gather(got_lists[None], 'latent', axis=0, tiled=True)  40.8 us
    all_gather x1, waiting for transfers between devices, shards(): lax.all_gather(got_rows[None], 'latent', axis=0, tiled=True)  24 us
    all_to_all x1, blocking collectives, shards(): lax.all_to_all(send_rows, 'expert', split_axis=0, concat_axis=0, tiled=True)  11.2 us
    dot_general x1, matrix products, shards(): jnp.dot(shifted, weights_here, preferred_element_type=jnp.float32)  8.73 us
  transfers between devices with their start and end apart: 3, of which 3 were waited for; matrix products, arithmetic and copies ran while one was open for 2% of the time, Pallas kernels for 0%

commit v1 on v0

--- a/solution.py
+++ b/solution.py
@@ -5,6 +5,11 @@
 
 BLK = 128
 CAP = 2
+
+
+def axis_by_axis(x, one, other):
+    half = lax.psum(x, one)
+    return lax.psum(half, other)
 
 
 def shards(tokens, route, blocks, weight, enc_bias, dec_bias):
@@ -71,7 +76,7 @@
     )
     bias_term = jnp.sum(error_share, axis=0) - pulled
     loss_term = 0.5 * jnp.sum(error_share * error_share)
-    grad_dec, loss_sum = lax.psum((bias_term, loss_term), ("expert", "latent"))
+    grad_dec, loss_sum = axis_by_axis((bias_term, loss_term), "latent", "expert")
     loss = loss_sum / (tokens.shape[0] * n_expert * n_latent)
     return (grad_here.astype(jnp.bfloat16)[None], grad_bias[None], grad_dec, loss)
 

time: 403 us -> 490 us (1.22)
  blocking collectives: 128 us -> 214 us
    psum x1 -> x2, blocking collectives: 75.9 us -> 162 us  [the longest x1 113 us: axis_by_axis(): half = lax.psum(x, one)]
  transfers between devices with their start and end apart: 3 -> 3, of which waited for: 3 -> 3; matrix products, arithmetic and copies ran while one was open for 2% -> 1% of each run, Pallas kernels for 0% -> 0%
where the time goes in v1:
time: 490 us; the launch traced here: 489 us
  blocking collectives  214 us (44%)
  waiting for transfers between devices  197 us (40%)
  matrix products  30.3 us (6%)
  between operations  16.7 us (3%)
  other arithmetic  14.6 us (3%)
  local copies, waits for them, and re-layouts  12 us (2%)
    psum x1, waiting for transfers between devices, shards(): summed = lax.psum(partial_sum, 'latent')  168 us
    psum x1, blocking collectives, axis_by_axis(): half = lax.psum(x, one)  113 us
    psum x1, blocking collectives, axis_by_axis(): return lax.psum(half, other)  49.1 us
    all_gather x1, blocking collectives, shards(): lax.all_gather(got_lists[None], 'latent', axis=0, tiled=True)  40.8 us
    all_gather x1, waiting for transfers between devices, shards(): lax.all_gather(got_rows[None], 'latent', axis=0, tiled=True)  24 us
    all_to_all x1, blocking collectives, shards(): lax.all_to_all(send_rows, 'expert', split_axis=0, concat_axis=0, tiled=True)  11.2 us
  transfers between devices with their start and end apart: 3, of which 3 were waited for; matrix products, arithmetic and copies ran while one was open for 1% of the time, Pallas kernels for 0%

profile of v1, /device:TPU:1, one launch (start us, length us, event | category | flops | bytes accessed | tf_op | source)
XLA Modules:
  0.0 488.5 jit_solution(2492645457196000848)
XLA Ops:
  7.2 0.7 fusion.24
  8.0 0.8 select_reduce_fusion
  8.8 0.7 fusion.25
  9.5 0.9 scatter_custom_fusion
  10.4 11.2 %all_to_all.10 = bf16[8,2,2560]{2,1,0:T(2,128)(2,1)} all-to-all(bf16[8,2,2560]{2,1,0:T(2,128)(2,1)S(1)} %reshape.33), channel_id=1, replica_groups=mesh['expert'=8,'latent'=32] {'expert'}, dimensions={0} | all-to-all | bytes 163840 | tf_op jit(solution)/shard_map/all_to_all | solution.py:31
  21.7 0.8 scatter_custom_fusion.1
  22.4 0.7 reshape.68
  23.1 4.0 all-to-all-start.1
  27.1 4.5 all-to-all-done.1
  31.6 0.5 broadcast.43
  32.2 0.7 reduce.4
  32.9 40.8 %all-gather.1 = s32[256,2,64]{2,1,0:T(2,128)S(1)} all-gather(s32[8,2,64]{2,1,0:T(2,128)S(1)} %reshape.69), channel_id=3, replica_groups=mesh['expert'=8,'latent'=32] {'latent'}, dimensions={0}, use_global_device_ids=true | all-gather | bytes 135168 | tf_op jit(solution)/shard_map/all_gather | solution.py:36
  73.8 0.2 compare_reduce_fusion
  74.2 24.0 %all-gather.4.cloned.1.call-done = bf16[256,2,2560]{2,1,0:T(2,128)(2,1)} async-done(((bf16[8,2,2560]{2,1,0:T(2,128)(2,1)}), bf16[256,2,2560]{2,1,0:T(2,128)(2,1)}) %all-gather.4.cloned.1.call-update) | async-done | bytes 2621456 | tf_op jit(solution)/shard_map/all_gather | solution.py:35
  98.1 3.5 convert_element_type.56
  101.7 2.3 subtract_convert_fusion
  104.0 2.6 convert_element_type.47
  106.6 0.6 broadcast_in_dim.32
  107.3 8.7 %fusion.11 = (bf16[512,1024]{1,0:T(8,128)(2,1)S(1)}, f32[512,1024]{1,0:T(8,128)}) fusion(f32[64,8,8,128]{3,2,1,0:T(8,128)S(1)} %bitcast.51, f32[1024]{0:T(1024)S(1)} %bitcast.57, bf16[512,2560]{1,0:T(8,128)(2,1)} %convert_element_type.47, bf16[1,2560,1024]{2,1,0:T(8,128)(2,1)} %param.9), kind=kOutput, calls=%fused_computation.19 | convolution fusion | flops 2686451712 | bytes 13111296 | tf_op jit(solution)/shard_map/dot_general | solution.py:50
  116.0 1.0 copy-done.3
  117.0 4.7 fusion.4
  121.8 1.6 copy-done
  123.4 2.9 reshape.36
  126.4 168.2 %all-reduce.4.cloned.1.call-done = f32[512,2560]{1,0:T(8,128)} async-done(((f32[512,2560]{1,0:T(8,128)}), f32[512,2560]{1,0:T(8,128)}) %all-reduce.4.cloned.1.call-update) | async-done | bytes 5242896 | tf_op jit(solution)/shard_map/psum | solution.py:59
  294.5 4.9 %subtract_multiply_fusion = f32[512,2560]{1,0:T(8,128)S(1)} fusion(f32[512,2560]{1,0:T(8,128)} %reshape.36, f32[512,2560]{1,0:T(8,128)} %all-reduce.4.cloned.1.call-done, f32[512]{0:T(512)S(1)} %convert_reduce_fusion, f32[2560]{0:T(1024)S(1)} %copy-done.4), kind=kLoop, calls=%fused_computation.11 | loop fusion | flops 3932160 | bytes 15740928 | tf_op jit(solution)/shard_map/mul | solution.py:60
  299.5 5.9 %fusion.26 = (f32[1024]{0:T(1024)S(1)}, bf16[512,1024]{1,0:T(8,128)(2,1)S(1)}) fusion(f32[64,8,8,128]{3,2,1,0:T(8,128)S(1)} %bitcast.52, bf16[1,2560,1024]{2,1,0:T(8,128)(2,1)} %param.9, f32[512,2560]{1,0:T(8,128)S(1)} %subtract_multiply_fusion, f32[512,1024]{1,0:T(8,128)S(1)} %copy-done.7, f32[1024]{0:T(1024)S(1)} %bitcast.58), kind=kOutput, calls=%fused_computation.40 | convolution fusion | flops 2688809984 | bytes 15736832 | tf_op jit(solution)/shard_map/dot_general | solution.py:63
  305.5 3.0 fusion.9
  308.5 6.5 %fusion.8 = bf16[1,2560,1024]{2,1,0:T(8,128)(2,1)} fusion(f32[2560,1024]{1,0:T(8,128)S(1)} %fusion.9, bf16[512,1024]{1,0:T(8,128)(2,1)} %copy-done.3, f32[512,2560]{1,0:T(8,128)S(1)} %subtract_multiply_fusion), kind=kOutput, calls=%fused_computation.14 | convolution fusion | flops 2690908160 | bytes 22020096 | tf_op jit(solution)/shard_map/dot_general | solution.py:70
  315.0 0.6 multiply_reduce_fusion
  315.6 1.5 fusion.16
  317.8 113.0 %all-reduce = (f32[2560]{0:T(1024)S(1)}, f32[]{:T(128)}) all-reduce(f32[2560]{0:T(1024)S(1)} %sub.28, f32[]{:T(128)S(6)} %mul_shard_map.3), channel_id=1, replica_groups=mesh['expert'=8,'latent'=32] {'latent'}, use_global_device_ids=true, to_apply=%region_8.9 | all-reduce | flops 2561 | bytes 20488 | tf_op jit(solution)/shard_map/psum | solution.py:11
  430.8 49.1 %all-reduce.1 = (f32[2560]{0:T(1024)}, f32[]{:T(128)}) all-reduce(f32[2560]{0:T(1024)S(1)} %get-tuple-element.6, f32[]{:T(128)} %get-tuple-element.7), channel_id=1, replica_groups=mesh['expert'=8,'latent'=32] {'expert'}, use_global_device_ids=true, to_apply=%region_9.10 | all-reduce | flops 2561 | bytes 20488 | tf_op jit(solution)/shard_map/psum | solution.py:12
  (44 shorter events, 0.7 us)
Async XLA Ops:
  7.2 94.5 %copy-start.4 = (f32[2560]{0:T(1024)S(1)}, f32[2560]{0:T(1024)}, u32[]{:S(2)}) copy-start(f32[2560]{0:T(1024)} %param.11) | copy-start | bytes 30724
  7.2 91.0 %all-gather.4.cloned.1.call-start = ((), (), s32[]{:S(2)}) async-start(), calls=%async_computation.3 | async-start | bytes 2703360 | tf_op jit(solution)/shard_map/all_gather | solution.py:35
  23.1 8.5 %all-to-all-start.1 = ((s32[8,1,128]{2,1,0:T(1,128)}), s32[8,1,128]{2,1,0:T(1,128)S(1)}, u32[]{:S(2)}, u32[]{:S(2)}) async-start(s32[8,1,128]{2,1,0:T(1,128)} %reshape.68), calls=%async_computation.1 | async-start | bytes 8192 | tf_op jit(solution)/shard_map/all_to_all | solution.py:32
  27.1 267.4 %all-reduce.4.cloned.1.call-start = ((), (), s32[]{:S(2)}) async-start(), calls=%async_computation.2 | async-start | bytes 10485760 | tf_op jit(solution)/shard_map/psum | solution.py:59
  104.0 3.2 copy-start.6
  106.6 10.4 %slice-start.2 = ((s8[5242880]{0:T(1024)(128)(4,1)}), s8[4194304]{0:T(1024)(128)(4,1)S(1)}, s32[]{:S(2)}) async-start(s8[5242880]{0:T(1024)(128)(4,1)} %bitcast.45), calls=%async_computation.6 | async-start | bytes 8388608
  107.2 8.8 %copy-start.1 = (f32[512,8,128]{2,1,0:T(8,128)}, f32[512,8,128]{2,1,0:T(8,128)S(1)}, u32[]{:S(2)}) copy-start(f32[512,8,128]{2,1,0:T(8,128)S(1)} %broadcast_in_dim.32) | copy-start | bytes 6291460
  107.2 9.7 %slice-start.3 = ((s8[5242880]{0:T(1024)(128)(4,1)}), s8[1048576]{0:T(1024)(128)(4,1)S(1)}, s32[]{:S(2)}) async-start(s8[5242880]{0:T(1024)(128)(4,1)} %bitcast.45), calls=%async_computation.7 | async-start | bytes 2097152
  116.0 1.0 copy-start.3
  121.7 1.7 copy-start
  126.3 173.1 %copy-start.2 = (f32[512,8,128]{2,1,0:T(8,128)S(1)}, f32[512,8,128]{2,1,0:T(8,128)}, u32[]{:S(2)}) copy-start(f32[512,8,128]{2,1,0:T(8,128)} %copy-done.1) | copy-start | bytes 6291460
  294.5 4.9 %copy-start.7 = (f32[512,1024]{1,0:T(8,128)S(1)}, f32[512,1024]{1,0:T(8,128)}, u32[]{:S(2)}) copy-start(f32[512,1024]{1,0:T(8,128)} %get-tuple-element.11) | copy-start | bytes 6291460
  294.5 10.9 %slice-start = ((s8[5242880]{0:T(1024)(128)(4,1)}), s8[1048576]{0:T(1024)(128)(4,1)S(1)}, s32[]{:S(2)}) async-start(s8[5242880]{0:T(1024)(128)(4,1)} %bitcast.42), calls=%async_computation.4 | async-start | bytes 2097152
  299.5 6.0 %slice-start.1 = ((s8[5242880]{0:T(1024)(128)(4,1)}), s8[4194304]{0:T(1024)(128)(4,1)S(1)}, s32[]{:S(2)}) async-start(s8[5242880]{0:T(1024)(128)(4,1)} %bitcast.42), calls=%async_computation.5 | async-start | bytes 8388608
  305.4 10.2 %copy-start.5 = (f32[1024]{0:T(1024)}, f32[1024]{0:T(1024)S(1)}, u32[]{:S(2)}) copy-start(f32[1024]{0:T(1024)S(1)} %get-tuple-element.12) | copy-start | bytes 12292
  305.4 10.2 %slice-start.4 = ((s8[5242880]{0:T(1024)(128)(4,1)}), s8[4194304]{0:T(1024)(128)(4,1)S(1)}, s32[]{:S(2)}) async-start(s8[5242880]{0:T(1024)(128)(4,1)} %bitcast.47), calls=%async_computation.8 | async-start | bytes 8388608
  308.5 7.2 %slice-start.5 = ((s8[5242880]{0:T(1024)(128)(4,1)}), s8[1048576]{0:T(1024)(128)(4,1)S(1)}, s32[]{:S(2)}) async-start(s8[5242880]{0:T(1024)(128)(4,1)} %bitcast.47), calls=%async_computation.9 | async-start | bytes 2097152
Sparse Core Ops, SparseCore 0:
  21.8 76.3 all-gather.3
  121.8 172.6 all-reduce.3
